TPU v7x, 32 devices: a whole 2x2x4 slice. The times are simulated.
32 devices in a mesh: gx: 4 (over y, x), gy: 8 (over z, core).
Axes of the slice: x: 2, y: 2, z: 4, core: 2. Of those that a mesh axis runs over, the one named last changes fastest.
Arguments:
- schur: float32 [4, 8, 512, 512], P('gx', 'gy'), may hold values from -1 to 25, as said below
- precond: float32 [4, 8, 512, 512], P('gx', 'gy'), may hold values from -1 to 25, as said below
- loads: float32 [4, 8, 512, 256], P('gx', 'gy'), may hold values from -12 to 12
- coarse_inv: float32 [128, 128], P('gx'), may hold values from -1 to 25, as said below
- edge_rows: int32 [4, 8, 512], P('gx', 'gy'), may hold values from 0 to 511, each once within a row
- corner_rows: int32 [4, 8, 4], P('gx', 'gy'), may hold values from 0 to 511, as said below
Outputs:
- multipliers: float32 [4, 8, 512, 256], P('gx', 'gy')
- residual: float32 [4, 8, 512, 256], P('gx', 'gy')
Inputs may be any that keep to these rules, and one draw needn't show every extreme that they name: `edge_rows`: for every subdomain the 512 entries name each local interface row once. `corner_rows`: local interface rows of each subdomain's 4 corner modes; entries of one subdomain may repeat. `schur`: every subdomain's block is symmetric positive definite. `precond`: every subdomain's block is symmetric positive definite. `coarse_inv`: symmetric positive definite; row and column (i * 8 + j) * 4 + m belong to mode m of subdomain (i, j).
All inputs are finite; a program needn't handle non-finite values.
Results may differ from a plain program's by a relative error of at most 0.00017.
Values sent between devices are 32-bit elements; how exact they have to be, the bound alone decides.
No kernel may reach another device: no remote copies, remote signals or barrier semaphores. Data moves between devices by JAX's collectives and lax.ppermute only.
A program may use at most 64 MiB of HBM per device.

v0:
```python
import jax
import jax.numpy as jnp
from jax import lax
from jax.sharding import PartitionSpec as P

MODES = 4
ITERS = 2


highest = lax.Precision.HIGHEST


def with_halo(cells, sides, width):
    for axis, dim in sides:
        count = lax.axis_size(axis)
        head = lax.slice_in_dim(cells, 0, width, axis=dim)
        tail = lax.slice_in_dim(cells, cells.shape[dim] - width, cells.shape[dim], axis=dim)
        cells = jnp.concatenate(
            [
                lax.ppermute(tail, axis, [(i, (i + 1) % count) for i in range(count)]),
                cells,
                lax.ppermute(head, axis, [((i + 1) % count, i) for i in range(count)]),
            ],
            axis=dim,
        )
    return cells


def matmul(first_op, second_op):
    return jnp.dot(first_op, second_op, precision=highest, preferred_element_type=jnp.float32)


def edge_jumps(source, local_rows, inverse):
    edge_size = local_rows.shape[0] // 4
    picked = jnp.take(source, local_rows, axis=0).reshape(4, edge_size, source.shape[1])
    across = with_halo(picked[0:2], (("gx", 0),), 1)
    upward = with_halo(picked[2:4], (("gy", 0),), 1)
    west_jump = picked[0] - across[0]
    east_jump = picked[1] - across[3]
    south_jump = picked[2] - upward[0]
    north_jump = picked[3] - upward[3]
    stacked = jnp.stack([west_jump, east_jump, south_jump, north_jump]).reshape(source.shape)
    return jnp.take(stacked, inverse, axis=0)


def coarse_by_column(corner_res, coarse_inv, grid_row):
    across_count = lax.axis_size("gx")
    along_count = lax.axis_size("gy")
    column_res = lax.all_gather(corner_res, "gx", axis=0, tiled=True)
    group_rows = coarse_inv.shape[0]
    shaped = coarse_inv.reshape(group_rows, across_count, along_count, MODES)
    chosen = lax.dynamic_slice_in_dim(shaped, grid_row, 1, 2).reshape(
        group_rows, across_count * MODES
    )
    return lax.psum_scatter(matmul(chosen, column_res), "gy", scatter_dimension=0, tiled=True)


def on_device(schur, precond, loads, coarse_inv, edge_rows, corner_rows):
    schur_block = schur[0, 0]
    precond_block = precond[0, 0]
    local_loads = loads[0, 0]
    local_rows = edge_rows[0, 0]
    corner_local = corner_rows[0, 0]
    row_total = local_rows.shape[0]
    positions = jnp.arange(row_total, dtype=jnp.int32)
    inverse = jnp.zeros((row_total,), jnp.int32).at[local_rows].set(positions)
    corner_pick = (corner_local[:, None] == positions[None, :]).astype(jnp.float32)
    grid_row = lax.axis_index("gy")
    dual_rhs = edge_jumps(local_loads, local_rows, inverse)
    multipliers = jnp.zeros_like(dual_rhs)
    residual = dual_rhs
    for iteration in range(ITERS):
        corner_res = matmul(corner_pick, residual)
        coarse_sol = coarse_by_column(corner_res, coarse_inv, grid_row)
        lifted = 0.25 * matmul(precond_block, residual) + matmul(corner_pick.T, coarse_sol)
        search = edge_jumps(lifted, local_rows, inverse)
        schur_image = matmul(schur_block, search)
        numerator = lax.psum(jnp.sum(residual * search, axis=0), ("gx", "gy"))
        dual_image = edge_jumps(schur_image, local_rows, inverse)
        denominator = lax.psum(jnp.sum(search * dual_image, axis=0), ("gx", "gy"))
        step_size = numerator / denominator
        multipliers = multipliers + step_size * search
        residual = residual - step_size * dual_image
    return (multipliers[None, None], residual[None, None])


def solution(mesh):
    in_specs = (
        P("gx", "gy", None, None),
        P("gx", "gy", None, None),
        P("gx", "gy", None, None),
        P("gx", None),
        P("gx", "gy", None),
        P("gx", "gy", None),
    )
    out_specs = (P("gx", "gy", None, None), P("gx", "gy", None, None))
    return jax.shard_map(
        on_device, mesh=mesh, in_specs=in_specs, out_specs=out_specs, check_vma=False
    )
```

profile of v0, /device:TPU:0, one launch (start us, length us, event | category | flops | bytes accessed | tf_op | source)
XLA Modules:
  0.0 237.3 jit_solution(15812877509895643523)
XLA Ops:
  1.5 2.6 %gather_fusion = f32[512,256]{1,0:T(8,128)S(1)} fusion(f32[512,256]{1,0:T(8,128)} %bitcast.136, s32[1024]{0:T(1024)S(1)} %pad_clamp_fusion.1), kind=kCustom, calls=%fused_computation.clone | custom fusion | bytes 1050624 | tf_op jit(solution)/shard_map/jit(_take)/gather | solution.py:35
  4.3 3.0 %collective-permute-start = (f32[1,128,256]{2,1,0:T(8,128)S(1)}, f32[1,128,256]{2,1,0:T(8,128)S(1)}, u32[]{:S(2)}, u32[]{:S(2)}) collective-permute-start(f32[1,128,256]{2,1,0:T(8,128)S(1)} %get-tuple-element.47), channel_id=1, source_target_pairs={{0,8},{8,16},{16,24},{24,0},{1,9},{9,17},{17,25},{25,1},{2,10},{10... | collective-permute-start | bytes 393224 | tf_op jit(solution)/shard_map/ppermute | solution.py:20
  7.3 3.5 %collective-permute-start.3 = (f32[1,128,256]{2,1,0:T(8,128)S(1)}, f32[1,128,256]{2,1,0:T(8,128)S(1)}, u32[]{:S(2)}, u32[]{:S(2)}) collective-permute-start(f32[1,128,256]{2,1,0:T(8,128)S(1)} %get-tuple-element.49), channel_id=1, source_target_pairs={{1,0},{2,1},{3,2},{4,3},{5,4},{6,5},{7,6},{0,7},{9,8},{10,9},{11,1... | collective-permute-start | bytes 393224 | tf_op jit(solution)/shard_map/ppermute | solution.py:22
  11.9 2.4 %scatter_custom_fusion = s32[512]{0:T(512)S(1)} fusion(s32[512]{0:T(512)S(1)} %bitcast.146, s32[512]{0:T(512)S(1)} %iota.6, s32[]{:T(128)} %constant.1.clone.1), kind=kCustom, calls=%fused_computation.90 | custom fusion | bytes 2052 | tf_op jit(solution)/shard_map/scatter | solution.py:66
  19.1 8.6 %all-gather = f32[4,4,256]{2,1,0:T(4,128)S(1)} all-gather(f32[1,4,256]{2,1,0:T(4,128)S(1)} %convolution_bitcast_fusion.3), channel_id=1, replica_groups=mesh['gx'=4,'gy'=8] {'gx'}, dimensions={0}, use_global_device_ids=true | all-gather | bytes 20480 | tf_op jit(solution)/shard_map/all_gather | solution.py:49
  28.0 25.9 %all-reduce = f32[32,256]{1,0:T(8,128)S(1)} all-reduce(f32[32,256]{1,0:T(8,128)S(1)} %fusion.56), channel_id=2, replica_groups=mesh['gx'=4,'gy'=8] {'gy'}, use_global_device_ids=true, to_apply=%region_1.0.clone | all-reduce | flops 8192 | bytes 65536
  54.4 2.0 fusion.2
  59.0 3.5 %collective-permute-start.7 = (f32[1,128,256]{2,1,0:T(8,128)S(1)}, f32[1,128,256]{2,1,0:T(8,128)S(1)}, u32[]{:S(2)}, u32[]{:S(2)}) collective-permute-start(f32[1,128,256]{2,1,0:T(8,128)S(1)} %get-tuple-element.41), channel_id=1, source_target_pairs={{1,0},{2,1},{3,2},{4,3},{5,4},{6,5},{7,6},{0,7},{9,8},{10,9},{11,1... | collective-permute-start | bytes 393224 | tf_op jit(solution)/shard_map/ppermute | solution.py:22
  62.6 2.3 collective-permute-start.5
  65.6 1.9 collective-permute-done.5
  69.2 3.2 %convolution_bitcast_fusion.1 = f32[512,256]{0,1:T(8,128)S(1)} fusion(f32[1,1,512,512]{3,2,1,0:T(8,128)} %param.8, f32[512,256]{1,0:T(8,128)S(1)} %gather_fusion.3, pred[512]{0:T(512)(128)(4,1)S(1)} %compare_and_fusion), kind=kOutput, calls=%fused_computation.18 | convolution fusion | flops 805437440 | bytes 2097664 | tf_op jit(solution)/shard_map/dot_general | solution.py:30
  72.6 1.6 gather_fusion.4
  74.4 2.4 %collective-permute-start.8 = (f32[1,128,256]{2,1,0:T(8,128)S(1)}, f32[1,128,256]{2,1,0:T(8,128)S(1)}, u32[]{:S(2)}, u32[]{:S(2)}) collective-permute-start(f32[1,128,256]{2,1,0:T(8,128)S(1)} %get-tuple-element.31), channel_id=1, source_target_pairs={{0,8},{8,16},{16,24},{24,0},{1,9},{9,17},{17,25},{25,1},{2,10},{10... | collective-permute-start | bytes 393224 | tf_op jit(solution)/shard_map/ppermute | solution.py:20
  76.8 3.5 %collective-permute-start.11 = (f32[1,128,256]{2,1,0:T(8,128)S(1)}, f32[1,128,256]{2,1,0:T(8,128)S(1)}, u32[]{:S(2)}, u32[]{:S(2)}) collective-permute-start(f32[1,128,256]{2,1,0:T(8,128)S(1)} %get-tuple-element.33), channel_id=1, source_target_pairs={{1,0},{2,1},{3,2},{4,3},{5,4},{6,5},{7,6},{0,7},{9,8},{10,9},{11,1... | collective-permute-start | bytes 393224 | tf_op jit(solution)/shard_map/ppermute | solution.py:22
  81.3 1.7 collective-permute-done.10
  83.0 2.3 collective-permute-done.9
  85.4 1.6 gather_fusion.5
  87.2 37.4 %all-reduce.3 = (f32[256]{0:T(256)S(1)}, f32[256]{0:T(256)S(1)}) all-reduce(f32[256]{0:T(256)S(1)} %get-tuple-element.6, f32[256]{0:T(256)S(1)} %get-tuple-element.5), channel_id=1, replica_groups=mesh['gx'=4,'gy'=8] {'gx','gy'}, use_global_device_ids=true, to_apply=%region_3.5 | all-reduce | flops 512 | bytes 4096 | tf_op jit(solution)/shard_map/psum | solution.py:78
  125.1 9.0 %all-gather.1 = f32[4,4,256]{2,1,0:T(4,128)S(1)} all-gather(f32[1,4,256]{2,1,0:T(4,128)S(1)} %convolution_bitcast_fusion.2), channel_id=1, replica_groups=mesh['gx'=4,'gy'=8] {'gx'}, dimensions={0}, use_global_device_ids=true | all-gather | bytes 20480 | tf_op jit(solution)/shard_map/all_gather | solution.py:49
  134.3 25.9 %all-reduce.1 = f32[32,256]{1,0:T(8,128)S(1)} all-reduce(f32[32,256]{1,0:T(8,128)S(1)} %fusion.57), channel_id=3, replica_groups=mesh['gx'=4,'gy'=8] {'gy'}, use_global_device_ids=true, to_apply=%region_6.8.clone | all-reduce | flops 8192 | bytes 65536
  160.7 1.9 fusion.3
  165.7 3.5 %collective-permute-start.15 = (f32[1,128,256]{2,1,0:T(8,128)S(1)}, f32[1,128,256]{2,1,0:T(8,128)S(1)}, u32[]{:S(2)}, u32[]{:S(2)}) collective-permute-start(f32[1,128,256]{2,1,0:T(8,128)S(1)} %get-tuple-element.25), channel_id=1, source_target_pairs={{1,0},{2,1},{3,2},{4,3},{5,4},{6,5},{7,6},{0,7},{9,8},{10,9},{11,1... | collective-permute-start | bytes 393224 | tf_op jit(solution)/shard_map/ppermute | solution.py:22
  169.3 1.8 collective-permute-start.13
  171.9 2.3 collective-permute-done.13
  175.9 4.0 %convolution_bitcast_fusion = f32[512,256]{0,1:T(8,128)} fusion(f32[1,1,512,512]{3,2,1,0:T(8,128)} %param.8, f32[512,256]{1,0:T(8,128)S(1)} %gather_fusion.7, pred[512]{0:T(512)(128)(4,1)S(1)} %compare_and_fusion), kind=kOutput, calls=%fused_computation.17 | convolution fusion | flops 805437440 | bytes 2097664 | tf_op jit(solution)/shard_map/dot_general | solution.py:30
  181.2 2.2 gather_fusion.8
  184.6 2.4 %collective-permute-start.16 = (f32[1,128,256]{2,1,0:T(8,128)S(1)}, f32[1,128,256]{2,1,0:T(8,128)S(1)}, u32[]{:S(2)}, u32[]{:S(2)}) collective-permute-start(f32[1,128,256]{2,1,0:T(8,128)S(1)} %get-tuple-element.15), channel_id=1, source_target_pairs={{0,8},{8,16},{16,24},{24,0},{1,9},{9,17},{17,25},{25,1},{2,10},{10... | collective-permute-start | bytes 393224 | tf_op jit(solution)/shard_map/ppermute | solution.py:20
  187.0 3.5 %collective-permute-start.19 = (f32[1,128,256]{2,1,0:T(8,128)S(1)}, f32[1,128,256]{2,1,0:T(8,128)S(1)}, u32[]{:S(2)}, u32[]{:S(2)}) collective-permute-start(f32[1,128,256]{2,1,0:T(8,128)S(1)} %get-tuple-element.17), channel_id=1, source_target_pairs={{1,0},{2,1},{3,2},{4,3},{5,4},{6,5},{7,6},{0,7},{9,8},{10,9},{11,1... | collective-permute-start | bytes 393224 | tf_op jit(solution)/shard_map/ppermute | solution.py:22
  191.1 2.1 collective-permute-done.18
  193.2 2.3 collective-permute-done.17
  195.7 2.2 gather_fusion.9
  199.2 36.9 %all-reduce.2 = (f32[256]{0:T(256)S(1)}, f32[256]{0:T(256)S(1)}) all-reduce(f32[256]{0:T(256)S(1)} %get-tuple-element.4, f32[256]{0:T(256)S(1)} %get-tuple-element.3), channel_id=1, replica_groups=mesh['gx'=4,'gy'=8] {'gx','gy'}, use_global_device_ids=true, to_apply=%region_8.10 | all-reduce | flops 512 | bytes 4096 | tf_op jit(solution)/shard_map/psum | solution.py:78
  (90 shorter events, 25.7 us)
Async XLA Ops:
  0.6 53.8 %copy-start = (f32[1,1,512,512]{3,2,1,0:T(8,128)S(1)}, f32[1,1,512,512]{3,2,1,0:T(8,128)}, u32[]{:S(2)}) copy-start(f32[1,1,512,512]{3,2,1,0:T(8,128)} %param.9) | copy-start | bytes 3145732
  0.6 0.8 copy-start.2
  4.3 12.1 %collective-permute-start = (f32[1,128,256]{2,1,0:T(8,128)S(1)}, f32[1,128,256]{2,1,0:T(8,128)S(1)}, u32[]{:S(2)}, u32[]{:S(2)}) collective-permute-start(f32[1,128,256]{2,1,0:T(8,128)S(1)} %get-tuple-element.47), channel_id=1, source_target_pairs={{0,8},{8,16},{16,24},{24,0},{1,9},{9,17},{17,25},{25,1},{2,10},{10... | collective-permute-start | bytes 393224 | tf_op jit(solution)/shard_map/ppermute | solution.py:20
  7.3 9.1 %collective-permute-start.2 = (f32[1,128,256]{2,1,0:T(8,128)S(1)}, f32[1,128,256]{2,1,0:T(8,128)S(1)}, u32[]{:S(2)}, u32[]{:S(2)}) collective-permute-start(f32[1,128,256]{2,1,0:T(8,128)S(1)} %get-tuple-element.48), channel_id=1, source_target_pairs={{0,1},{1,2},{2,3},{3,4},{4,5},{5,6},{6,7},{7,0},{8,9},{9,10},{10,1... | collective-permute-start | bytes 393224 | tf_op jit(solution)/shard_map/ppermute | solution.py:20
  7.3 9.1 %collective-permute-start.3 = (f32[1,128,256]{2,1,0:T(8,128)S(1)}, f32[1,128,256]{2,1,0:T(8,128)S(1)}, u32[]{:S(2)}, u32[]{:S(2)}) collective-permute-start(f32[1,128,256]{2,1,0:T(8,128)S(1)} %get-tuple-element.49), channel_id=1, source_target_pairs={{1,0},{2,1},{3,2},{4,3},{5,4},{6,5},{7,6},{0,7},{9,8},{10,9},{11,1... | collective-permute-start | bytes 393224 | tf_op jit(solution)/shard_map/ppermute | solution.py:22
  10.8 5.6 %collective-permute-start.1 = (f32[1,128,256]{2,1,0:T(8,128)S(1)}, f32[1,128,256]{2,1,0:T(8,128)S(1)}, u32[]{:S(2)}, u32[]{:S(2)}) collective-permute-start(f32[1,128,256]{2,1,0:T(8,128)S(1)} %get-tuple-element.50), channel_id=1, source_target_pairs={{8,0},{16,8},{24,16},{0,24},{9,1},{17,9},{25,17},{1,25},{10,2},{18... | collective-permute-start | bytes 393224 | tf_op jit(solution)/shard_map/ppermute | solution.py:22
  11.9 2.5 %copy-start.3 = (f32[32,128]{1,0:T(8,128)S(1)}, f32[32,128]{1,0:T(8,128)}, u32[]{:S(2)}) copy-start(f32[32,128]{1,0:T(8,128)} %param.11) | copy-start | bytes 49156
  14.5 0.7 copy-start.5
  18.1 0.7 copy-start.4
  58.4 7.2 %collective-permute-start.4 = (f32[1,128,256]{2,1,0:T(8,128)S(1)}, f32[1,128,256]{2,1,0:T(8,128)S(1)}, u32[]{:S(2)}, u32[]{:S(2)}) collective-permute-start(f32[1,128,256]{2,1,0:T(8,128)S(1)} %get-tuple-element.39), channel_id=1, source_target_pairs={{0,8},{8,16},{16,24},{24,0},{1,9},{9,17},{17,25},{25,1},{2,10},{10... | collective-permute-start | bytes 393224 | tf_op jit(solution)/shard_map/ppermute | solution.py:20
  59.0 6.6 %collective-permute-start.6 = (f32[1,128,256]{2,1,0:T(8,128)S(1)}, f32[1,128,256]{2,1,0:T(8,128)S(1)}, u32[]{:S(2)}, u32[]{:S(2)}) collective-permute-start(f32[1,128,256]{2,1,0:T(8,128)S(1)} %get-tuple-element.40), channel_id=1, source_target_pairs={{0,1},{1,2},{2,3},{3,4},{4,5},{5,6},{6,7},{7,0},{8,9},{9,10},{10,1... | collective-permute-start | bytes 393224 | tf_op jit(solution)/shard_map/ppermute | solution.py:20
  59.0 6.6 %collective-permute-start.7 = (f32[1,128,256]{2,1,0:T(8,128)S(1)}, f32[1,128,256]{2,1,0:T(8,128)S(1)}, u32[]{:S(2)}, u32[]{:S(2)}) collective-permute-start(f32[1,128,256]{2,1,0:T(8,128)S(1)} %get-tuple-element.41), channel_id=1, source_target_pairs={{1,0},{2,1},{3,2},{4,3},{5,4},{6,5},{7,6},{0,7},{9,8},{10,9},{11,1... | collective-permute-start | bytes 393224 | tf_op jit(solution)/shard_map/ppermute | solution.py:22
  62.6 5.0 %collective-permute-start.5 = (f32[1,128,256]{2,1,0:T(8,128)S(1)}, f32[1,128,256]{2,1,0:T(8,128)S(1)}, u32[]{:S(2)}, u32[]{:S(2)}) collective-permute-start(f32[1,128,256]{2,1,0:T(8,128)S(1)} %get-tuple-element.42), channel_id=1, source_target_pairs={{8,0},{16,8},{24,16},{0,24},{9,1},{17,9},{25,17},{1,25},{10,2},{18... | collective-permute-start | bytes 393224 | tf_op jit(solution)/shard_map/ppermute | solution.py:22
  74.4 6.9 %collective-permute-start.8 = (f32[1,128,256]{2,1,0:T(8,128)S(1)}, f32[1,128,256]{2,1,0:T(8,128)S(1)}, u32[]{:S(2)}, u32[]{:S(2)}) collective-permute-start(f32[1,128,256]{2,1,0:T(8,128)S(1)} %get-tuple-element.31), channel_id=1, source_target_pairs={{0,8},{8,16},{16,24},{24,0},{1,9},{9,17},{17,25},{25,1},{2,10},{10... | collective-permute-start | bytes 393224 | tf_op jit(solution)/shard_map/ppermute | solution.py:20
  76.8 6.2 %collective-permute-start.10 = (f32[1,128,256]{2,1,0:T(8,128)S(1)}, f32[1,128,256]{2,1,0:T(8,128)S(1)}, u32[]{:S(2)}, u32[]{:S(2)}) collective-permute-start(f32[1,128,256]{2,1,0:T(8,128)S(1)} %get-tuple-element.32), channel_id=1, source_target_pairs={{0,1},{1,2},{2,3},{3,4},{4,5},{5,6},{6,7},{7,0},{8,9},{9,10},{10,1... | collective-permute-start | bytes 393224 | tf_op jit(solution)/shard_map/ppermute | solution.py:20
  76.8 6.2 %collective-permute-start.11 = (f32[1,128,256]{2,1,0:T(8,128)S(1)}, f32[1,128,256]{2,1,0:T(8,128)S(1)}, u32[]{:S(2)}, u32[]{:S(2)}) collective-permute-start(f32[1,128,256]{2,1,0:T(8,128)S(1)} %get-tuple-element.33), channel_id=1, source_target_pairs={{1,0},{2,1},{3,2},{4,3},{5,4},{6,5},{7,6},{0,7},{9,8},{10,9},{11,1... | collective-permute-start | bytes 393224 | tf_op jit(solution)/shard_map/ppermute | solution.py:22
  80.4 5.0 %collective-permute-start.9 = (f32[1,128,256]{2,1,0:T(8,128)S(1)}, f32[1,128,256]{2,1,0:T(8,128)S(1)}, u32[]{:S(2)}, u32[]{:S(2)}) collective-permute-start(f32[1,128,256]{2,1,0:T(8,128)S(1)} %get-tuple-element.34), channel_id=1, source_target_pairs={{8,0},{16,8},{24,16},{0,24},{9,1},{17,9},{25,17},{1,25},{10,2},{18... | collective-permute-start | bytes 393224 | tf_op jit(solution)/shard_map/ppermute | solution.py:22
  164.6 7.2 %collective-permute-start.12 = (f32[1,128,256]{2,1,0:T(8,128)S(1)}, f32[1,128,256]{2,1,0:T(8,128)S(1)}, u32[]{:S(2)}, u32[]{:S(2)}) collective-permute-start(f32[1,128,256]{2,1,0:T(8,128)S(1)} %get-tuple-element.23), channel_id=1, source_target_pairs={{0,8},{8,16},{16,24},{24,0},{1,9},{9,17},{17,25},{25,1},{2,10},{10... | collective-permute-start | bytes 393224 | tf_op jit(solution)/shard_map/ppermute | solution.py:20
  165.7 6.2 %collective-permute-start.14 = (f32[1,128,256]{2,1,0:T(8,128)S(1)}, f32[1,128,256]{2,1,0:T(8,128)S(1)}, u32[]{:S(2)}, u32[]{:S(2)}) collective-permute-start(f32[1,128,256]{2,1,0:T(8,128)S(1)} %get-tuple-element.24), channel_id=1, source_target_pairs={{0,1},{1,2},{2,3},{3,4},{4,5},{5,6},{6,7},{7,0},{8,9},{9,10},{10,1... | collective-permute-start | bytes 393224 | tf_op jit(solution)/shard_map/ppermute | solution.py:20
  165.7 6.2 %collective-permute-start.15 = (f32[1,128,256]{2,1,0:T(8,128)S(1)}, f32[1,128,256]{2,1,0:T(8,128)S(1)}, u32[]{:S(2)}, u32[]{:S(2)}) collective-permute-start(f32[1,128,256]{2,1,0:T(8,128)S(1)} %get-tuple-element.25), channel_id=1, source_target_pairs={{1,0},{2,1},{3,2},{4,3},{5,4},{6,5},{7,6},{0,7},{9,8},{10,9},{11,1... | collective-permute-start | bytes 393224 | tf_op jit(solution)/shard_map/ppermute | solution.py:22
  169.3 5.0 %collective-permute-start.13 = (f32[1,128,256]{2,1,0:T(8,128)S(1)}, f32[1,128,256]{2,1,0:T(8,128)S(1)}, u32[]{:S(2)}, u32[]{:S(2)}) collective-permute-start(f32[1,128,256]{2,1,0:T(8,128)S(1)} %get-tuple-element.26), channel_id=1, source_target_pairs={{8,0},{16,8},{24,16},{0,24},{9,1},{17,9},{25,17},{1,25},{10,2},{18... | collective-permute-start | bytes 393224 | tf_op jit(solution)/shard_map/ppermute | solution.py:22
  184.6 6.5 %collective-permute-start.16 = (f32[1,128,256]{2,1,0:T(8,128)S(1)}, f32[1,128,256]{2,1,0:T(8,128)S(1)}, u32[]{:S(2)}, u32[]{:S(2)}) collective-permute-start(f32[1,128,256]{2,1,0:T(8,128)S(1)} %get-tuple-element.15), channel_id=1, source_target_pairs={{0,8},{8,16},{16,24},{24,0},{1,9},{9,17},{17,25},{25,1},{2,10},{10... | collective-permute-start | bytes 393224 | tf_op jit(solution)/shard_map/ppermute | solution.py:20
  187.0 6.2 %collective-permute-start.18 = (f32[1,128,256]{2,1,0:T(8,128)S(1)}, f32[1,128,256]{2,1,0:T(8,128)S(1)}, u32[]{:S(2)}, u32[]{:S(2)}) collective-permute-start(f32[1,128,256]{2,1,0:T(8,128)S(1)} %get-tuple-element.16), channel_id=1, source_target_pairs={{0,1},{1,2},{2,3},{3,4},{4,5},{5,6},{6,7},{7,0},{8,9},{9,10},{10,1... | collective-permute-start | bytes 393224 | tf_op jit(solution)/shard_map/ppermute | solution.py:20
  187.0 6.2 %collective-permute-start.19 = (f32[1,128,256]{2,1,0:T(8,128)S(1)}, f32[1,128,256]{2,1,0:T(8,128)S(1)}, u32[]{:S(2)}, u32[]{:S(2)}) collective-permute-start(f32[1,128,256]{2,1,0:T(8,128)S(1)} %get-tuple-element.17), channel_id=1, source_target_pairs={{1,0},{2,1},{3,2},{4,3},{5,4},{6,5},{7,6},{0,7},{9,8},{10,9},{11,1... | collective-permute-start | bytes 393224 | tf_op jit(solution)/shard_map/ppermute | solution.py:22
  190.6 5.0 %collective-permute-start.17 = (f32[1,128,256]{2,1,0:T(8,128)S(1)}, f32[1,128,256]{2,1,0:T(8,128)S(1)}, u32[]{:S(2)}, u32[]{:S(2)}) collective-permute-start(f32[1,128,256]{2,1,0:T(8,128)S(1)} %get-tuple-element.18), channel_id=1, source_target_pairs={{8,0},{16,8},{24,16},{0,24},{9,1},{17,9},{25,17},{1,25},{10,2},{18... | collective-permute-start | bytes 393224 | tf_op jit(solution)/shard_map/ppermute | solution.py:22
  197.9 38.2 %copy-start.1 = (f32[512,256]{1,0:T(8,128)S(1)}, f32[512,256]{1,0:T(8,128)}, u32[]{:S(2)}) copy-start(f32[512,256]{1,0:T(8,128)} %gather_fusion.9) | copy-start | bytes 1572868
where the time goes:
time: 238 us; the launch traced here: 237 us
  blocking collectives  144 us (61%)
  starting transfers between devices  34 us (14%)
  local copies, waits for them, and re-layouts  24.6 us (10%)
  waiting for transfers between devices  14.2 us (6%)
  matrix products  13 us (5%)
  other arithmetic  5.92 us (2%)
    psum x2, blocking collectives, on_device(): numerator = lax.psum(jnp.sum(residual * search, axis=0), ('gx', 'gy'))  74.3 us
    unnamed x2, blocking collectives  51.9 us
    ppermute x10, starting transfers between devices, with_halo(): lax.ppermute(head, axis, [((i + 1) % count, i) for i in range(count)])  24.4 us
    all_gather x2, blocking collectives, coarse_by_column(): column_res = lax.all_gather(corner_res, 'gx', axis=0, tiled=True)  17.6 us
    dot_general x10, matrix products, matmul(): jnp.dot(first_op, second_op, precision=highest, preferred_element_type=jn...  13 us
    ppermute x10, starting transfers between devices, with_halo(): lax.ppermute(tail, axis, [(i, (i + 1) % count) for i in range(count)])  9.65 us
    gather x5, local copies, waits for them, and re-layouts, edge_jumps(): jnp.take(source, local_rows, axis=0).reshape(4, edge_size, source.shape[1])  9.57 us
    ppermute x10, waiting for transfers between devices, with_halo(): lax.ppermute(head, axis, [((i + 1) % count, i) for i in range(count)])  8.9 us
  transfers between devices with their start and end apart: 20, of which 9 were waited for; matrix products, arithmetic and copies ran while one was open for 1% of the time, Pallas kernels for 0%

commit v1 on v0

v1 whole, which is shorter than its diff:
```python
import jax
import jax.numpy as jnp
from jax import lax
from jax.experimental import pallas as pl
from jax.experimental.pallas import tpu as pltpu
from jax.sharding import PartitionSpec as P

ITERS = 2
F32 = jnp.float32
BF16 = jnp.bfloat16
SUBLANES = 8


def halves(x):
    high = x.astype(BF16)
    return high, (x - high.astype(F32)).astype(BF16)


def thirds(x):
    high, rest = x.astype(BF16), None
    rest = x - high.astype(F32)
    middle, low = halves(rest)
    return high, middle, low


def dot(a, b):
    return jnp.dot(a, b, preferred_element_type=F32)


def dot_split(a_high, a_low, b):
    b_high, b_low = halves(b)
    return dot(a_high, b_high) + (dot(a_high, b_low) + dot(a_low, b_high))


def dot_exact(pick, x):
    high, middle, low = thirds(x)
    return dot(pick, high) + (dot(pick, middle) + dot(pick, low))


def one_hot_rows(rows_col, order):
    lanes = lax.broadcasted_iota(jnp.int32, (rows_col.shape[0], order), 1)
    return (rows_col == lanes).astype(F32).astype(BF16)


def one_hot_cols(rows_row, order):
    sublanes = lax.broadcasted_iota(jnp.int32, (order, rows_row.shape[1]), 0)
    return (rows_row == sublanes).astype(F32).astype(BF16)


def call(body, name, outs, args, flops=0, scalars=()):
    vmem = pl.BlockSpec(memory_space=pltpu.VMEM)
    smem = pl.BlockSpec(memory_space=pltpu.SMEM)
    moved = sum(a.size * a.dtype.itemsize for a in args)
    return pl.pallas_call(
        body,
        name=name,
        out_shape=[jax.ShapeDtypeStruct(s, d) for s, d in outs],
        in_specs=[smem] * len(scalars) + [vmem] * len(args),
        out_specs=[vmem] * len(outs),
        cost_estimate=pl.CostEstimate(flops=flops, bytes_accessed=moved, transcendentals=0),
        compiler_params=pltpu.CompilerParams(vmem_limit_bytes=24 * 1024 * 1024),
    )(*scalars, *args)


def gather_body(modes, edge, cases):
    def body(place, rows_col, corner_col, rows_row, loads, coarse, *outs):
        payloads, corner_out = outs[:4], outs[4]
        order = loads.shape[0]
        moved = dot_exact(one_hot_rows(rows_col[...], order), loads[...])
        corner = (corner_col[...] == rows_row[...]).astype(F32)
        corner_out[...] = corner
        own = [coarse[pl.ds(place[0] * modes + m, 1), :] for m in range(modes)]
        own = jnp.concatenate(own, axis=0)
        for k, out in enumerate(payloads):
            out[:edge, :] = moved[k * edge : (k + 1) * edge]
            info = jnp.concatenate([corner[:modes, k * edge : (k + 1) * edge], own], axis=1)
            for g in range((out.shape[0] - edge) // SUBLANES):
                part = info[:, g * cases : (g + 1) * cases]
                out[edge + g * SUBLANES : edge + g * SUBLANES + modes, : part.shape[1]] = part
    return body


def permute_body(rows_col, rows_row, block, high_out, low_out):
    order = block.shape[0]
    left = one_hot_rows(rows_col[...], order)
    right = one_hot_cols(rows_row[...], order)
    for part, out in zip(halves(block[...]), (high_out, low_out)):
        out[...] = dot(left, dot(part, right).astype(BF16)).astype(BF16)


def coarse_body(modes, edge, cases, devices):
    def body(mine0, mine1, mine2, mine3, his0, his1, his2, his3, high_out, low_out):
        total = devices * modes

        def info(ref):
            groups = (ref.shape[0] - edge) // SUBLANES
            parts = [
                ref[edge + g * SUBLANES : edge + g * SUBLANES + modes, :] for g in range(groups)
            ]
            whole = jnp.concatenate(parts, axis=1)
            return whole[:, :edge], whole[:, edge : edge + total]

        before = lax.broadcasted_iota(jnp.int32, (total, total), 0)
        after = lax.broadcasted_iota(jnp.int32, (total, total), 1)
        mode = jnp.zeros_like(after)
        for m in range(1, modes):
            mode = mode + (after >= m * devices).astype(jnp.int32)
        shuffle = (before == (after - mode * devices) * modes + mode).astype(F32).astype(BF16)
        for k, (mine, his) in enumerate(zip((mine0, mine1, mine2, mine3), (his0, his1, his2, his3))):
            my_pick, my_rows = info(mine)
            his_pick, his_rows = info(his)
            picks = jnp.concatenate([my_pick, -his_pick], axis=0).astype(BF16)
            rows = jnp.concatenate([my_rows, his_rows], axis=0)
            shuffled = dot_exact_right(rows, shuffle)
            high, low = [], None
            spread = sum(
                lax.dot_general(
                    picks, part, (((0,), (0,)), ((), ())), preferred_element_type=F32
                )
                for part in thirds(shuffled)
            )
            high, low = halves(spread)
            high_out[k * edge : (k + 1) * edge, :] = high
            low_out[k * edge : (k + 1) * edge, :] = low
    return body


def dot_exact_right(x, pick):
    high, middle, low = thirds(x)
    return dot(high, pick) + (dot(middle, pick) + dot(low, pick))


def solution(mesh):
    across, along = mesh.shape["gx"], mesh.shape["gy"]
    devices = across * along
    axes = ("gx", "gy")

    def ring_pairs(count, odd):
        pairs = []
        for first in range(odd, count + odd, 2):
            a, b = first % count, (first + 1) % count
            pairs += [(a, b), (b, a)]
        return pairs

    routes = (
        ("gx", ring_pairs(across, 0)),
        ("gx", ring_pairs(across, 1)),
        ("gy", ring_pairs(along, 0)),
        ("gy", ring_pairs(along, 1)),
    )

    def swap(parts):
        return [lax.ppermute(part, axis, pairs) for part, (axis, pairs) in zip(parts, routes)]

    def to_all(x):
        return lax.all_to_all(x, axes, 0, 0)

    def on_device(schur, precond, loads, coarse_inv, edge_rows, corner_rows):
        schur, precond, loads = schur[0, 0], precond[0, 0], loads[0, 0]
        order, cases = loads.shape
        modes = corner_rows.shape[2]
        edge = order // 4
        i, j = lax.axis_index("gx"), lax.axis_index("gy")
        west, east, south, north = jnp.split(edge_rows[0, 0], 4)
        even_i, even_j = i % 2 == 0, j % 2 == 0
        rows = jnp.concatenate(
            [
                jnp.where(even_i, east, west),
                jnp.where(even_i, west, east),
                jnp.where(even_j, north, south),
                jnp.where(even_j, south, north),
            ]
        )
        rows_col, rows_row = rows[:, None], rows[None, :]
        corner_col = jnp.concatenate(
            [corner_rows[0, 0], jnp.full((SUBLANES - modes,), -1, jnp.int32)]
        )[:, None]
        place = j.astype(jnp.int32).reshape(1)
        total = devices * modes
        groups = -(-(edge + total) // cases)
        payload_rows = edge + groups * SUBLANES
        mat = 2 * order * order * cases

        *payloads, corner = call(
            gather_body(modes, edge, cases),
            "gather",
            [((payload_rows, cases), F32)] * 4 + [((SUBLANES, order), F32)],
            (rows_col, corner_col, rows_row, loads, coarse_inv),
            3 * mat,
            (place,),
        )
        got = swap(payloads)
        pre_high, pre_low = call(
            permute_body, "permute_precond", [((order, order), BF16)] * 2,
            (rows_col, rows_row, precond), 8 * order**3,
        )
        sch_high, sch_low = call(
            permute_body, "permute_schur", [((order, order), BF16)] * 2,
            (rows_col, rows_row, schur), 8 * order**3,
        )
        mode_high, mode_low = call(
            coarse_body(modes, edge, cases, devices), "coarse_map",
            [((order, total), BF16)] * 2, (*payloads, *got),
        )

        def jump(mine, his):
            return jnp.concatenate([a[:edge, :] - b[:edge, :] for a, b in zip(mine, his)], axis=0)

        def put(outs, x):
            for k, out in enumerate(outs):
                out[...] = x[k * edge : (k + 1) * edge]

        def gathered(ref):
            return jnp.concatenate([ref[:, m, :] for m in range(modes)], axis=0)

        edges = [((edge, cases), F32)] * 4
        field = [((order, cases), F32)]

        def second(*refs):
            mine, his = refs[0:4], refs[4:8]
            high, low, pick, residual_out = refs[8:12]
            outs, sent = refs[12:16], refs[16]
            residual = jump(mine, his)
            residual_out[...] = residual
            put(outs, 0.25 * dot_split(high[...], low[...], residual))
            sent[...] = jnp.broadcast_to(
                dot_exact(pick[...].astype(BF16), residual)[None, :modes], sent.shape
            )

        residual, *lifted, sent = call(
            second, "apply_precond_0", field + edges + [((devices, modes, cases), F32)],
            (*payloads, *got, pre_high, pre_low, corner), 3 * mat,
        )
        got = swap(lifted)
        coarse = to_all(sent)

        def third(*refs):
            mine, his = refs[0:4], refs[4:8]
            coarse, m_high, m_low, high, low, search_out = refs[8:14]
            search = jump(mine, his) + dot_split(m_high[...], m_low[...], gathered(coarse))
            search_out[...] = search
            put(refs[14:18], dot_split(high[...], low[...], search))

        search, *image = call(
            third, "apply_schur_0", field + edges,
            (*lifted, *got, coarse, mode_high, mode_low, sch_high, sch_low), 3 * mat,
        )
        got = swap(image)

        def fourth(*refs):
            mine, his = refs[0:4], refs[4:8]
            residual, search, high, low, pick, dual_out = refs[8:14]
            outs, sent = refs[14:18], refs[18]
            dual = jump(mine, his)
            dual_out[...] = dual
            put(outs, 0.25 * dot_split(high[...], low[...], dual))
            rows = [
                dot_exact(pick[...].astype(BF16), dual)[:modes],
                jnp.sum(residual[...] * search[...], axis=0, keepdims=True),
                jnp.sum(search[...] * dual, axis=0, keepdims=True),
            ]
            sent[...] = jnp.broadcast_to(jnp.concatenate(rows, axis=0)[None], sent.shape)

        dual, *lifted, sent = call(
            fourth, "apply_precond_1", field + edges + [((devices, modes + 2, cases), F32)],
            (*image, *got, residual, search, pre_high, pre_low, corner), 3 * mat,
        )
        got = swap(lifted)
        coarse = to_all(sent)

        def fifth(*refs):
            mine, his = refs[0:4], refs[4:8]
            coarse, m_high, m_low, high, low = refs[8:13]
            image = refs[13:17]
            residual, search, dual, next_out, step_out = refs[17:22]
            outs, sent = refs[22:26], refs[26]
            change = jump(mine, his) + dot_split(m_high[...], m_low[...], gathered(coarse))
            change_image = dot_split(high[...], low[...], change)
            put(outs, change_image)
            step = jnp.sum(coarse[:, modes, :], axis=0, keepdims=True) / jnp.sum(
                coarse[:, modes + 1, :], axis=0, keepdims=True
            )
            step_out[...] = step
            following = search[...] - step * change
            next_out[...] = following
            schur_image = jnp.concatenate([x[...] for x in image], axis=0) - step * change_image
            rows = [
                jnp.sum((residual[...] - step * dual[...]) * following, axis=0, keepdims=True),
                2.0 * jnp.sum(following * schur_image, axis=0, keepdims=True),
            ]
            sent[...] = jnp.broadcast_to(jnp.concatenate(rows, axis=0)[None], sent.shape)

        following, step, *change_image, sent = call(
            fifth, "apply_schur_1",
            field + [((1, cases), F32)] + edges + [((devices, 2, cases), F32)],
            (*lifted, *got, coarse, mode_high, mode_low, sch_high, sch_low, *image,
             residual, search, dual), 3 * mat,
        )
        got = swap(change_image)
        sums = to_all(sent)

        def last(*refs):
            mine, his = refs[0:4], refs[4:8]
            sums, step, rows_row, residual, search, dual, following, mult_out, res_out = refs[8:]
            back = one_hot_cols(rows_row[...], order)
            step, dual = step[...], dual[...]
            final = jnp.sum(sums[:, 0, :], axis=0, keepdims=True) / jnp.sum(
                sums[:, 1, :], axis=0, keepdims=True
            )
            mult_out[...] = dot_exact(back, step * search[...] + final * following[...])
            new_dual = dual - step * jump(mine, his)
            res_out[...] = dot_exact(back, residual[...] - step * dual - final * new_dual)

        multipliers, residual = call(
            last, "finish", field * 2,
            (*change_image, *got, sums, step, rows_row, residual, search, dual, following), 6 * mat,
        )
        return multipliers[None, None], residual[None, None]

    in_specs = (
        P("gx", "gy", None, None),
        P("gx", "gy", None, None),
        P("gx", "gy", None, None),
        P("gx", None),
        P("gx", "gy", None),
        P("gx", "gy", None),
    )
    out_specs = (P("gx", "gy", None, None), P("gx", "gy", None, None))
    return jax.shard_map(
        on_device, mesh=mesh, in_specs=in_specs, out_specs=out_specs, check_vma=False
    )
```

time: 238 us -> 102 us (0.43)
  blocking collectives: 144 us -> 9.28 us
  matrix products: 13 us -> 0 us
  Pallas kernels: 0 us -> 12.7 us
  other arithmetic: 5.92 us -> 0.72 us
  starting transfers between devices: 34 us -> 37.8 us
  local copies, waits for them, and re-layouts: 24.6 us -> 27.5 us
    psum x2 -> x0, blocking collectives: 74.3 us -> none  [on_device(): numerator = lax.psum(jnp.sum(residual * search, axis=0), ('gx', 'gy'))]
    unnamed x2 -> x0, blocking collectives: 51.9 us -> none
    unnamed x16 -> x88, local copies, waits for them, and re-layouts: 2.02 us -> 26.5 us
    gather x10 -> x0, local copies, waits for them, and re-layouts: 18.1 us -> none  [the longest x5 9.57 us: edge_jumps(): jnp.take(source, local_rows, axis=0).reshape(4, edge_size, source.shape[1])]
    all_gather x2 -> x0, blocking collectives: 17.6 us -> none  [coarse_by_column(): column_res = lax.all_gather(corner_res, 'gx', axis=0, tiled=True)]
    dot_general x10 -> x0, matrix products: 13 us -> none  [matmul(): jnp.dot(first_op, second_op, precision=highest, preferred_element_type=jn...]
    pallas_call x0 -> x9, Pallas kernels: none -> 12.7 us  [call(): pl.pallas_call(body, name=name, out_shape=[jax.ShapeDtypeStruct(s, d) for...]
    all_to_all x0 -> x1, blocking collectives: none -> 9.28 us  [to_all(): return lax.all_to_all(x, axes, 0, 0)]
  transfers between devices with their start and end apart: 20 -> 22, of which waited for: 9 -> 7; matrix products, arithmetic and copies ran while one was open for 1% -> 0% of each run, Pallas kernels for 0% -> 4%
where the time goes in v1:
time: 102 us; the launch traced here: 101 us
  starting transfers between devices  37.8 us (37%)
  local copies, waits for them, and re-layouts  27.5 us (27%)
  Pallas kernels  12.7 us (12%)
  waiting for transfers between devices  12 us (12%)
  blocking collectives  9.28 us (9%)
    ppermute x20, starting transfers between devices, swap(): lax.ppermute(part, axis, pairs)  30.7 us
    unnamed x88, local copies, waits for them, and re-layouts  26.5 us
    pallas_call x9, Pallas kernels, call(): pl.pallas_call(body, name=name, out_shape=[jax.ShapeDtypeStruct(s, d) for...  12.7 us
    ppermute x20, waiting for transfers between devices, swap(): lax.ppermute(part, axis, pairs)  12 us
    all_to_all x1, blocking collectives, to_all(): return lax.all_to_all(x, axes, 0, 0)  9.28 us
    all_to_all x2, starting transfers between devices, to_all(): return lax.all_to_all(x, axes, 0, 0)  7.18 us
  transfers between devices with their start and end apart: 22, of which 7 were waited for; matrix products, arithmetic and copies ran while one was open for 0% of the time, Pallas kernels for 4%

profile of v1, /device:TPU:0, one launch (start us, length us, event | category | flops | bytes accessed | tf_op | source)
XLA Modules:
  0.0 100.9 jit_solution(3847165317526344996)
XLA Ops:
  2.4 1.1 %copy-done.42 = f32[1,1,512,256]{3,2,1,0:T(8,128)S(1)} copy-done((f32[1,1,512,256]{3,2,1,0:T(8,128)S(1)}, f32[1,1,512,256]{3,2,1,0:T(8,128)}, u32[]{:S(2)}) %copy-start.42) | copy-done | bytes 524312
  4.9 3.0 %collective-permute-start = (f32[136,256]{1,0:T(8,128)S(1)}, f32[136,256]{1,0:T(8,128)S(1)}, u32[]{:S(2)}, u32[]{:S(2)}) collective-permute-start(f32[136,256]{1,0:T(8,128)S(1)} %get-tuple-element.39.refs_0_.mine0), channel_id=1, source_target_pairs={{0,8},{8,0},{16,24},{24,16},{1,9},{9,1},{17,25},{25,17},{2,10},{10... | collective-permute-start | bytes 417800 | tf_op jit(solution)/shard_map/ppermute | solution.py:153
  7.9 1.5 %collective-permute-start.1 = (f32[136,256]{1,0:T(8,128)S(1)}, f32[136,256]{1,0:T(8,128)S(1)}, u32[]{:S(2)}, u32[]{:S(2)}) collective-permute-start(f32[136,256]{1,0:T(8,128)S(1)} %get-tuple-element.40.refs_1_.mine1), channel_id=1, source_target_pairs={{8,16},{16,8},{24,0},{0,24},{9,17},{17,9},{25,1},{1,25},{10,18},{1... | collective-permute-start | bytes 417800 | tf_op jit(solution)/shard_map/ppermute | solution.py:153
  9.4 3.7 %collective-permute-start.3 = (f32[136,256]{1,0:T(8,128)S(1)}, f32[136,256]{1,0:T(8,128)S(1)}, u32[]{:S(2)}, u32[]{:S(2)}) collective-permute-start(f32[136,256]{1,0:T(8,128)S(1)} %get-tuple-element.42.refs_3_.mine3), channel_id=1, source_target_pairs={{1,2},{2,1},{3,4},{4,3},{5,6},{6,5},{7,0},{0,7},{9,10},{10,9},{11,... | collective-permute-start | bytes 417800 | tf_op jit(solution)/shard_map/ppermute | solution.py:153
  13.2 1.5 %permute_precond.1 = (bf16[512,512]{1,0:T(8,128)(2,1)S(1)}, bf16[512,512]{1,0:T(8,128)(2,1)S(1)}) custom-call(s32[512,1]{1,0:T(8,128)S(1)} %copy.9.rows_col, s32[1,512]{1,0:T(1,128)S(1)} %bitcast.21, f32[512,512]{1,0:T(8,128)S(1)} %bitcast.24), custom_call_target="tpu_custom_call" | custom-call | flops 1073741824 | bytes 1052672 | tf_op jit(solution)/shard_map/permute_precond/pallas_call | solution.py:54
  14.7 1.1 %collective-permute-done.1.refs_5_.his1 = f32[136,256]{1,0:T(8,128)S(1)} collective-permute-done((f32[136,256]{1,0:T(8,128)S(1)}, f32[136,256]{1,0:T(8,128)S(1)}, u32[]{:S(2)}, u32[]{:S(2)}) %collective-permute-start.1) | collective-permute-done | bytes 139296 | tf_op jit(solution)/shard_map/ppermute | solution.py:153
  16.6 1.4 %apply_precond_0.1 = (f32[512,256]{1,0:T(8,128)S(1)}, f32[128,256]{1,0:T(8,128)}, f32[128,256]{1,0:T(8,128)}, f32[128,256]{1,0:T(8,128)}, f32[128,256]{1,0:T(8,128)}, /*index=5*/f32[32,4,256]{2,1,0:T(4,128)}) custom-call(f32[136,256]{1,0:T(8,128)S(1)} %get-tuple-element.39.refs_0_.mine0, f32[136,256]{1,0:T(8,128)S(1)} %get-tuple-element.40.refs_1_.mine1, ...), custom_call_target="tpu_custom_call" | custom-call | flops 402653184 | bytes 2179072 | tf_op jit(solution)/shard_map/apply_precond_0/pallas_call | solution.py:54
  18.1 4.2 %all-to-all-start = ((f32[32,4,256]{2,1,0:T(4,128)}), f32[32,4,256]{2,1,0:T(4,128)}, u32[]{:S(2)}, u32[]{:S(2)}) async-start(f32[32,4,256]{2,1,0:T(4,128)} %get-tuple-element.50), calls=%async_computation | async-start | bytes 262144 | tf_op jit(solution)/shard_map/all_to_all | solution.py:156
  22.3 1.8 %collective-permute-start.4 = (f32[128,256]{1,0:T(8,128)}, f32[128,256]{1,0:T(8,128)S(1)}, u32[]{:S(2)}, u32[]{:S(2)}) collective-permute-start(f32[128,256]{1,0:T(8,128)} %get-tuple-element.46.refs_0_), channel_id=1, source_target_pairs={{0,8},{8,0},{16,24},{24,16},{1,9},{9,1},{17,25},{25,17},{2,10},{10... | collective-permute-start | bytes 393224 | tf_op jit(solution)/shard_map/ppermute | solution.py:153
  24.1 1.5 %collective-permute-start.5 = (f32[128,256]{1,0:T(8,128)}, f32[128,256]{1,0:T(8,128)S(1)}, u32[]{:S(2)}, u32[]{:S(2)}) collective-permute-start(f32[128,256]{1,0:T(8,128)} %get-tuple-element.47.refs_1_), channel_id=1, source_target_pairs={{8,16},{16,8},{24,0},{0,24},{9,17},{17,9},{25,1},{1,25},{10,18},{1... | collective-permute-start | bytes 393224 | tf_op jit(solution)/shard_map/ppermute | solution.py:153
  25.5 3.5 %collective-permute-start.7 = (f32[128,256]{1,0:T(8,128)}, f32[128,256]{1,0:T(8,128)S(1)}, u32[]{:S(2)}, u32[]{:S(2)}) collective-permute-start(f32[128,256]{1,0:T(8,128)} %get-tuple-element.49.refs_3_), channel_id=1, source_target_pairs={{1,2},{2,1},{3,4},{4,3},{5,6},{6,5},{7,0},{0,7},{9,10},{10,9},{11,... | collective-permute-start | bytes 393224 | tf_op jit(solution)/shard_map/ppermute | solution.py:153
  29.0 0.9 copy-done.10
  29.9 1.2 %copy-done.41 = f32[1,1,512,512]{3,2,1,0:T(8,128)S(1)} copy-done((f32[1,1,512,512]{3,2,1,0:T(8,128)S(1)}, f32[1,1,512,512]{3,2,1,0:T(8,128)}, u32[]{:S(2)}) %copy-start.41) | copy-done | bytes 1048600
  31.2 1.5 %permute_schur.1 = (bf16[512,512]{1,0:T(8,128)(2,1)S(1)}, bf16[512,512]{1,0:T(8,128)(2,1)S(1)}) custom-call(s32[512,1]{1,0:T(8,128)S(1)} %copy-done.10, s32[1,512]{1,0:T(1,128)S(1)} %bitcast.22, f32[512,512]{1,0:T(8,128)S(1)} %bitcast.25), custom_call_target="tpu_custom_call" | custom-call | flops 1073741824 | bytes 1052672 | tf_op jit(solution)/shard_map/permute_schur/pallas_call | solution.py:54
  41.3 2.5 %apply_schur_0.1 = (f32[512,256]{1,0:T(8,128)S(1)}, f32[128,256]{1,0:T(8,128)S(1)}, f32[128,256]{1,0:T(8,128)S(1)}, f32[128,256]{1,0:T(8,128)S(1)}, f32[128,256]{1,0:T(8,128)S(1)}) custom-call(f32[128,256]{1,0:T(8,128)} %get-tuple-element.46.refs_0_, f32[128,256]{1,0:T(8,128)} %get-tuple-element.47.refs_1_, f32[128,256]{1,0:T(8,128)} %get-tuple-element.48.refs_2_, ...), custom_call_target="tpu_custom_call" | custom-call | flops 402653184 | bytes 2490368 | tf_op jit(solution)/shard_map/apply_schur_0/pallas_call | solution.py:54
  43.8 1.5 %collective-permute-start.8 = (f32[128,256]{1,0:T(8,128)S(1)}, f32[128,256]{1,0:T(8,128)S(1)}, u32[]{:S(2)}, u32[]{:S(2)}) collective-permute-start(f32[128,256]{1,0:T(8,128)S(1)} %get-tuple-element.55.refs_0_.refs_13_), channel_id=1, source_target_pairs={{0,8},{8,0},{16,24},{24,16},{1,9},{9,1},{17,25},{25,17},{2,10},{10... | collective-permute-start | bytes 393224 | tf_op jit(solution)/shard_map/ppermute | solution.py:153
  45.9 1.6 %collective-permute-start.11 = (f32[128,256]{1,0:T(8,128)S(1)}, f32[128,256]{1,0:T(8,128)S(1)}, u32[]{:S(2)}, u32[]{:S(2)}) collective-permute-start(f32[128,256]{1,0:T(8,128)S(1)} %get-tuple-element.58.refs_3_.refs_16_), channel_id=1, source_target_pairs={{1,2},{2,1},{3,4},{4,3},{5,6},{6,5},{7,0},{0,7},{9,10},{10,9},{11,... | collective-permute-start | bytes 393224 | tf_op jit(solution)/shard_map/ppermute | solution.py:153
  47.5 1.4 %collective-permute-done.8.refs_4_ = f32[128,256]{1,0:T(8,128)S(1)} collective-permute-done((f32[128,256]{1,0:T(8,128)S(1)}, f32[128,256]{1,0:T(8,128)S(1)}, u32[]{:S(2)}, u32[]{:S(2)}) %collective-permute-start.8) | collective-permute-done | bytes 131104 | tf_op jit(solution)/shard_map/ppermute | solution.py:153
  48.9 2.4 %collective-permute-done.9.refs_5_ = f32[128,256]{1,0:T(8,128)S(1)} collective-permute-done((f32[128,256]{1,0:T(8,128)S(1)}, f32[128,256]{1,0:T(8,128)S(1)}, u32[]{:S(2)}, u32[]{:S(2)}) %collective-permute-start.9) | collective-permute-done | bytes 131104 | tf_op jit(solution)/shard_map/ppermute | solution.py:153
  51.3 1.3 %collective-permute-done.11.refs_7_ = f32[128,256]{1,0:T(8,128)S(1)} collective-permute-done((f32[128,256]{1,0:T(8,128)S(1)}, f32[128,256]{1,0:T(8,128)S(1)}, u32[]{:S(2)}, u32[]{:S(2)}) %collective-permute-start.11) | collective-permute-done | bytes 131104 | tf_op jit(solution)/shard_map/ppermute | solution.py:153
  56.6 3.0 %all-to-all-start.1 = ((f32[32,6,256]{2,1,0:T(8,128)}), f32[32,6,256]{2,1,0:T(8,128)S(1)}, u32[]{:S(2)}, u32[]{:S(2)}) async-start(f32[32,6,256]{2,1,0:T(8,128)} %copy-done.11), calls=%async_computation.1 | async-start | bytes 524288 | tf_op jit(solution)/shard_map/all_to_all | solution.py:156
  59.6 1.8 %collective-permute-start.12 = (f32[128,256]{1,0:T(8,128)}, f32[128,256]{1,0:T(8,128)S(1)}, u32[]{:S(2)}, u32[]{:S(2)}) collective-permute-start(f32[128,256]{1,0:T(8,128)} %copy-done.12), channel_id=1, source_target_pairs={{0,8},{8,0},{16,24},{24,16},{1,9},{9,1},{17,25},{25,17},{2,10},{10... | collective-permute-start | bytes 393224 | tf_op jit(solution)/shard_map/ppermute | solution.py:153
  61.4 1.5 %collective-permute-start.13 = (f32[128,256]{1,0:T(8,128)}, f32[128,256]{1,0:T(8,128)S(1)}, u32[]{:S(2)}, u32[]{:S(2)}) collective-permute-start(f32[128,256]{1,0:T(8,128)} %copy-done.14), channel_id=1, source_target_pairs={{8,16},{16,8},{24,0},{0,24},{9,17},{17,9},{25,1},{1,25},{10,18},{1... | collective-permute-start | bytes 393224 | tf_op jit(solution)/shard_map/ppermute | solution.py:153
  62.9 3.5 %collective-permute-start.15 = (f32[128,256]{1,0:T(8,128)}, f32[128,256]{1,0:T(8,128)S(1)}, u32[]{:S(2)}, u32[]{:S(2)}) collective-permute-start(f32[128,256]{1,0:T(8,128)} %copy-done.18), channel_id=1, source_target_pairs={{1,2},{2,1},{3,4},{4,3},{5,6},{6,5},{7,0},{0,7},{9,10},{10,9},{11,... | collective-permute-start | bytes 393224 | tf_op jit(solution)/shard_map/ppermute | solution.py:153
  66.4 1.6 %collective-permute-done.12.refs_4_ = f32[128,256]{1,0:T(8,128)S(1)} collective-permute-done((f32[128,256]{1,0:T(8,128)}, f32[128,256]{1,0:T(8,128)S(1)}, u32[]{:S(2)}, u32[]{:S(2)}) %collective-permute-start.12) | collective-permute-done | bytes 131104 | tf_op jit(solution)/shard_map/ppermute | solution.py:153
  68.6 3.3 %collective-permute-done.13.refs_5_ = f32[128,256]{1,0:T(8,128)S(1)} collective-permute-done((f32[128,256]{1,0:T(8,128)}, f32[128,256]{1,0:T(8,128)S(1)}, u32[]{:S(2)}, u32[]{:S(2)}) %collective-permute-start.13) | collective-permute-done | bytes 131104 | tf_op jit(solution)/shard_map/ppermute | solution.py:153
  82.0 1.4 %apply_schur_1.1 = (f32[512,256]{1,0:T(8,128)S(1)}, f32[1,256]{1,0:T(1,128)S(1)}, f32[128,256]{1,0:T(8,128)S(1)}, f32[128,256]{1,0:T(8,128)S(1)}, f32[128,256]{1...) custom-call(f32[128,256]{1,0:T(8,128)S(1)} %copy-done.13, f32[128,256]{1,0:T(8,128)S(1)} %copy-done.15, ...), custom_call_target="tpu_custom_call" | custom-call | flops 402653184 | bytes 4653056 | tf_op jit(solution)/shard_map/apply_schur_1/pallas_call | solution.py:54
  83.3 1.1 %collective-permute-start.16 = (f32[128,256]{1,0:T(8,128)S(1)}, f32[128,256]{1,0:T(8,128)S(1)}, u32[]{:S(2)}, u32[]{:S(2)}) collective-permute-start(f32[128,256]{1,0:T(8,128)S(1)} %get-tuple-element.67.refs_0_), channel_id=1, source_target_pairs={{0,8},{8,0},{16,24},{24,16},{1,9},{9,1},{17,25},{25,17},{2,10},{10... | collective-permute-start | bytes 393224 | tf_op jit(solution)/shard_map/ppermute | solution.py:153
  84.4 0.9 collective-permute-start.17
  85.3 3.4 %collective-permute-start.19 = (f32[128,256]{1,0:T(8,128)S(1)}, f32[128,256]{1,0:T(8,128)S(1)}, u32[]{:S(2)}, u32[]{:S(2)}) collective-permute-start(f32[128,256]{1,0:T(8,128)S(1)} %get-tuple-element.70.refs_3_), channel_id=1, source_target_pairs={{1,2},{2,1},{3,4},{4,3},{5,6},{6,5},{7,0},{0,7},{9,10},{10,9},{11,... | collective-permute-start | bytes 393224 | tf_op jit(solution)/shard_map/ppermute | solution.py:153
  88.7 9.3 %all_to_all.15.refs_8_ = f32[32,2,256]{2,1,0:T(2,128)S(1)} all-to-all(f32[32,2,256]{2,1,0:T(2,128)S(1)} %get-tuple-element.71), channel_id=1, replica_groups=mesh['gx'=4,'gy'=8] {'gx','gy'}, dimensions={0} | all-to-all | bytes 131072 | tf_op jit(solution)/shard_map/all_to_all | solution.py:156
  98.7 2.2 %finish.1 = (f32[512,256]{1,0:T(8,128)}, f32[512,256]{1,0:T(8,128)}) custom-call(f32[128,256]{1,0:T(8,128)S(1)} %get-tuple-element.67.refs_0_, f32[128,256]{1,0:T(8,128)S(1)} %get-tuple-element.68.refs_1_, f32[128,256]{1,0:T(8,128)S(1)} %get-tuple-element.69.refs_2_, f32[128,256]{1,0:T(8,128)S(1)} %get-tuple-element.70.refs_3_, ...), custom_call_target="tpu_custom_call" | custom-call | flops 805306368 | bytes 3214336 | tf_op jit(solution)/shard_map/finish/pallas_call | solution.py:54
  (115 shorter events, 28.5 us)
Async XLA Ops:
  0.6 12.5 %copy-start.40 = (f32[1,1,512,512]{3,2,1,0:T(8,128)S(1)}, f32[1,1,512,512]{3,2,1,0:T(8,128)}, u32[]{:S(2)}) copy-start(f32[1,1,512,512]{3,2,1,0:T(8,128)} %param.7) | copy-start | bytes 3145732
  2.2 26.8 %copy-start.38 = (s32[512]{0:T(512)}, s32[512]{0:T(512)S(1)}, u32[]{:S(2)}) copy-start(s32[512]{0:T(512)S(1)} %pad_add_fusion) | copy-start | bytes 6148
  2.4 10.8 %copy-start.9 = (s32[512,1]{1,0:T(8,128)}, s32[512,1]{1,0:T(8,128)S(1)}, u32[]{:S(2)}) copy-start(s32[512,1]{1,0:T(8,128)S(1)} %copy.9.rows_col) | copy-start | bytes 6148
  4.9 11.7 %copy-start.36 = (f32[8,512]{1,0:T(8,128)}, f32[8,512]{1,0:T(8,128)S(1)}, u32[]{:S(2)}) copy-start(f32[8,512]{1,0:T(8,128)S(1)} %get-tuple-element.45.refs_10_.refs_12_) | copy-start | bytes 49156
  4.9 9.7 %collective-permute-start = (f32[136,256]{1,0:T(8,128)S(1)}, f32[136,256]{1,0:T(8,128)S(1)}, u32[]{:S(2)}, u32[]{:S(2)}) collective-permute-start(f32[136,256]{1,0:T(8,128)S(1)} %get-tuple-element.39.refs_0_.mine0), channel_id=1, source_target_pairs={{0,8},{8,0},{16,24},{24,16},{1,9},{9,1},{17,25},{25,17},{2,10},{10... | collective-permute-start | bytes 417800 | tf_op jit(solution)/shard_map/ppermute | solution.py:153
  7.9 7.9 %collective-permute-start.1 = (f32[136,256]{1,0:T(8,128)S(1)}, f32[136,256]{1,0:T(8,128)S(1)}, u32[]{:S(2)}, u32[]{:S(2)}) collective-permute-start(f32[136,256]{1,0:T(8,128)S(1)} %get-tuple-element.40.refs_1_.mine1), channel_id=1, source_target_pairs={{8,16},{16,8},{24,0},{0,24},{9,17},{17,9},{25,1},{1,25},{10,18},{1... | collective-permute-start | bytes 417800 | tf_op jit(solution)/shard_map/ppermute | solution.py:153
  9.4 6.4 %collective-permute-start.2 = (f32[136,256]{1,0:T(8,128)S(1)}, f32[136,256]{1,0:T(8,128)S(1)}, u32[]{:S(2)}, u32[]{:S(2)}) collective-permute-start(f32[136,256]{1,0:T(8,128)S(1)} %get-tuple-element.41.refs_2_.mine2), channel_id=1, source_target_pairs={{0,1},{1,0},{2,3},{3,2},{4,5},{5,4},{6,7},{7,6},{8,9},{9,8},{10,11... | collective-permute-start | bytes 417800 | tf_op jit(solution)/shard_map/ppermute | solution.py:153
  9.4 7.2 %collective-permute-start.3 = (f32[136,256]{1,0:T(8,128)S(1)}, f32[136,256]{1,0:T(8,128)S(1)}, u32[]{:S(2)}, u32[]{:S(2)}) collective-permute-start(f32[136,256]{1,0:T(8,128)S(1)} %get-tuple-element.42.refs_3_.mine3), channel_id=1, source_target_pairs={{1,2},{2,1},{3,4},{4,3},{5,6},{6,5},{7,0},{0,7},{9,10},{10,9},{11,... | collective-permute-start | bytes 417800 | tf_op jit(solution)/shard_map/ppermute | solution.py:153
  18.1 18.7 %all-to-all-start = ((f32[32,4,256]{2,1,0:T(4,128)}), f32[32,4,256]{2,1,0:T(4,128)}, u32[]{:S(2)}, u32[]{:S(2)}) async-start(f32[32,4,256]{2,1,0:T(4,128)} %get-tuple-element.50), calls=%async_computation | async-start | bytes 262144 | tf_op jit(solution)/shard_map/all_to_all | solution.py:156
  22.3 11.9 %collective-permute-start.4 = (f32[128,256]{1,0:T(8,128)}, f32[128,256]{1,0:T(8,128)S(1)}, u32[]{:S(2)}, u32[]{:S(2)}) collective-permute-start(f32[128,256]{1,0:T(8,128)} %get-tuple-element.46.refs_0_), channel_id=1, source_target_pairs={{0,8},{8,0},{16,24},{24,16},{1,9},{9,1},{17,25},{25,17},{2,10},{10... | collective-permute-start | bytes 393224 | tf_op jit(solution)/shard_map/ppermute | solution.py:153
  24.1 10.8 %collective-permute-start.5 = (f32[128,256]{1,0:T(8,128)}, f32[128,256]{1,0:T(8,128)S(1)}, u32[]{:S(2)}, u32[]{:S(2)}) collective-permute-start(f32[128,256]{1,0:T(8,128)} %get-tuple-element.47.refs_1_), channel_id=1, source_target_pairs={{8,16},{16,8},{24,0},{0,24},{9,17},{17,9},{25,1},{1,25},{10,18},{1... | collective-permute-start | bytes 393224 | tf_op jit(solution)/shard_map/ppermute | solution.py:153
  25.5 10.0 %collective-permute-start.6 = (f32[128,256]{1,0:T(8,128)}, f32[128,256]{1,0:T(8,128)S(1)}, u32[]{:S(2)}, u32[]{:S(2)}) collective-permute-start(f32[128,256]{1,0:T(8,128)} %get-tuple-element.48.refs_2_), channel_id=1, source_target_pairs={{0,1},{1,0},{2,3},{3,2},{4,5},{5,4},{6,7},{7,6},{8,9},{9,8},{10,11... | collective-permute-start | bytes 393224 | tf_op jit(solution)/shard_map/ppermute | solution.py:153
  25.5 10.6 %collective-permute-start.7 = (f32[128,256]{1,0:T(8,128)}, f32[128,256]{1,0:T(8,128)S(1)}, u32[]{:S(2)}, u32[]{:S(2)}) collective-permute-start(f32[128,256]{1,0:T(8,128)} %get-tuple-element.49.refs_3_), channel_id=1, source_target_pairs={{1,2},{2,1},{3,4},{4,3},{5,6},{6,5},{7,0},{0,7},{9,10},{10,9},{11,... | collective-permute-start | bytes 393224 | tf_op jit(solution)/shard_map/ppermute | solution.py:153
  41.3 11.2 %copy-start.1 = (bf16[512,512]{1,0:T(8,128)(2,1)S(1)}, bf16[512,512]{1,0:T(8,128)(2,1)}, u32[]{:S(2)}) copy-start(bf16[512,512]{1,0:T(8,128)(2,1)} %copy-done) | copy-start | bytes 1572868
  41.3 11.2 %copy-start.37 = (f32[8,512]{1,0:T(8,128)S(1)}, f32[8,512]{1,0:T(8,128)}, u32[]{:S(2)}) copy-start(f32[8,512]{1,0:T(8,128)} %copy-done.36) | copy-start | bytes 49156
  43.8 9.5 %copy-start.5 = (f32[128,256]{1,0:T(8,128)}, f32[128,256]{1,0:T(8,128)S(1)}, u32[]{:S(2)}) copy-start(f32[128,256]{1,0:T(8,128)S(1)} %get-tuple-element.57.refs_2_.refs_15_) | copy-start | bytes 393220
  43.8 9.5 %copy-start.7 = (f32[128,256]{1,0:T(8,128)}, f32[128,256]{1,0:T(8,128)S(1)}, u32[]{:S(2)}) copy-start(f32[128,256]{1,0:T(8,128)S(1)} %get-tuple-element.58.refs_3_.refs_16_) | copy-start | bytes 393220
  43.8 5.0 %collective-permute-start.8 = (f32[128,256]{1,0:T(8,128)S(1)}, f32[128,256]{1,0:T(8,128)S(1)}, u32[]{:S(2)}, u32[]{:S(2)}) collective-permute-start(f32[128,256]{1,0:T(8,128)S(1)} %get-tuple-element.55.refs_0_.refs_13_), channel_id=1, source_target_pairs={{0,8},{8,0},{16,24},{24,16},{1,9},{9,1},{17,25},{25,17},{2,10},{10... | collective-permute-start | bytes 393224 | tf_op jit(solution)/shard_map/ppermute | solution.py:153
  45.4 5.9 %collective-permute-start.9 = (f32[128,256]{1,0:T(8,128)S(1)}, f32[128,256]{1,0:T(8,128)S(1)}, u32[]{:S(2)}, u32[]{:S(2)}) collective-permute-start(f32[128,256]{1,0:T(8,128)S(1)} %get-tuple-element.56.refs_1_.refs_14_), channel_id=1, source_target_pairs={{8,16},{16,8},{24,0},{0,24},{9,17},{17,9},{25,1},{1,25},{10,18},{1... | collective-permute-start | bytes 393224 | tf_op jit(solution)/shard_map/ppermute | solution.py:153
  45.9 5.3 %collective-permute-start.10 = (f32[128,256]{1,0:T(8,128)S(1)}, f32[128,256]{1,0:T(8,128)S(1)}, u32[]{:S(2)}, u32[]{:S(2)}) collective-permute-start(f32[128,256]{1,0:T(8,128)S(1)} %get-tuple-element.57.refs_2_.refs_15_), channel_id=1, source_target_pairs={{0,1},{1,0},{2,3},{3,2},{4,5},{5,4},{6,7},{7,6},{8,9},{9,8},{10,11... | collective-permute-start | bytes 393224 | tf_op jit(solution)/shard_map/ppermute | solution.py:153
  45.9 6.7 %collective-permute-start.11 = (f32[128,256]{1,0:T(8,128)S(1)}, f32[128,256]{1,0:T(8,128)S(1)}, u32[]{:S(2)}, u32[]{:S(2)}) collective-permute-start(f32[128,256]{1,0:T(8,128)S(1)} %get-tuple-element.58.refs_3_.refs_16_), channel_id=1, source_target_pairs={{1,2},{2,1},{3,4},{4,3},{5,6},{6,5},{7,0},{0,7},{9,10},{10,9},{11,... | collective-permute-start | bytes 393224 | tf_op jit(solution)/shard_map/ppermute | solution.py:153
  56.6 17.2 %copy-start.4 = (bf16[512,128]{1,0:T(8,128)(2,1)S(1)}, bf16[512,128]{1,0:T(8,128)(2,1)}, u32[]{:S(2)}) copy-start(bf16[512,128]{1,0:T(8,128)(2,1)} %copy-done.2) | copy-start | bytes 393220
  56.6 17.2 %copy-start.6 = (f32[128,256]{1,0:T(8,128)S(1)}, f32[128,256]{1,0:T(8,128)}, u32[]{:S(2)}) copy-start(f32[128,256]{1,0:T(8,128)} %copy-done.5) | copy-start | bytes 393220
  56.6 17.2 %all-to-all-start.1 = ((f32[32,6,256]{2,1,0:T(8,128)}), f32[32,6,256]{2,1,0:T(8,128)S(1)}, u32[]{:S(2)}, u32[]{:S(2)}) async-start(f32[32,6,256]{2,1,0:T(8,128)} %copy-done.11), calls=%async_computation.1 | async-start | bytes 524288 | tf_op jit(solution)/shard_map/all_to_all | solution.py:156
  59.6 8.3 %collective-permute-start.12 = (f32[128,256]{1,0:T(8,128)}, f32[128,256]{1,0:T(8,128)S(1)}, u32[]{:S(2)}, u32[]{:S(2)}) collective-permute-start(f32[128,256]{1,0:T(8,128)} %copy-done.12), channel_id=1, source_target_pairs={{0,8},{8,0},{16,24},{24,16},{1,9},{9,1},{17,25},{25,17},{2,10},{10... | collective-permute-start | bytes 393224 | tf_op jit(solution)/shard_map/ppermute | solution.py:153
  61.4 10.4 %collective-permute-start.13 = (f32[128,256]{1,0:T(8,128)}, f32[128,256]{1,0:T(8,128)S(1)}, u32[]{:S(2)}, u32[]{:S(2)}) collective-permute-start(f32[128,256]{1,0:T(8,128)} %copy-done.14), channel_id=1, source_target_pairs={{8,16},{16,8},{24,0},{0,24},{9,17},{17,9},{25,1},{1,25},{10,18},{1... | collective-permute-start | bytes 393224 | tf_op jit(solution)/shard_map/ppermute | solution.py:153
  62.9 9.6 %collective-permute-start.14 = (f32[128,256]{1,0:T(8,128)}, f32[128,256]{1,0:T(8,128)S(1)}, u32[]{:S(2)}, u32[]{:S(2)}) collective-permute-start(f32[128,256]{1,0:T(8,128)} %copy-done.16), channel_id=1, source_target_pairs={{0,1},{1,0},{2,3},{3,2},{4,5},{5,4},{6,7},{7,6},{8,9},{9,8},{10,11... | collective-permute-start | bytes 393224 | tf_op jit(solution)/shard_map/ppermute | solution.py:153
  62.9 10.3 %collective-permute-start.15 = (f32[128,256]{1,0:T(8,128)}, f32[128,256]{1,0:T(8,128)S(1)}, u32[]{:S(2)}, u32[]{:S(2)}) collective-permute-start(f32[128,256]{1,0:T(8,128)} %copy-done.18), channel_id=1, source_target_pairs={{1,2},{2,1},{3,4},{4,3},{5,6},{6,5},{7,0},{0,7},{9,10},{10,9},{11,... | collective-permute-start | bytes 393224 | tf_op jit(solution)/shard_map/ppermute | solution.py:153
  83.3 14.6 %collective-permute-start.16 = (f32[128,256]{1,0:T(8,128)S(1)}, f32[128,256]{1,0:T(8,128)S(1)}, u32[]{:S(2)}, u32[]{:S(2)}) collective-permute-start(f32[128,256]{1,0:T(8,128)S(1)} %get-tuple-element.67.refs_0_), channel_id=1, source_target_pairs={{0,8},{8,0},{16,24},{24,16},{1,9},{9,1},{17,25},{25,17},{2,10},{10... | collective-permute-start | bytes 393224 | tf_op jit(solution)/shard_map/ppermute | solution.py:153
  84.4 13.6 %collective-permute-start.17 = (f32[128,256]{1,0:T(8,128)S(1)}, f32[128,256]{1,0:T(8,128)S(1)}, u32[]{:S(2)}, u32[]{:S(2)}) collective-permute-start(f32[128,256]{1,0:T(8,128)S(1)} %get-tuple-element.68.refs_1_), channel_id=1, source_target_pairs={{8,16},{16,8},{24,0},{0,24},{9,17},{17,9},{25,1},{1,25},{10,18},{1... | collective-permute-start | bytes 393224 | tf_op jit(solution)/shard_map/ppermute | solution.py:153
  85.3 12.7 %collective-permute-start.18 = (f32[128,256]{1,0:T(8,128)S(1)}, f32[128,256]{1,0:T(8,128)S(1)}, u32[]{:S(2)}, u32[]{:S(2)}) collective-permute-start(f32[128,256]{1,0:T(8,128)S(1)} %get-tuple-element.69.refs_2_), channel_id=1, source_target_pairs={{0,1},{1,0},{2,3},{3,2},{4,5},{5,4},{6,7},{7,6},{8,9},{9,8},{10,11... | collective-permute-start | bytes 393224 | tf_op jit(solution)/shard_map/ppermute | solution.py:153
  85.3 12.7 %collective-permute-start.19 = (f32[128,256]{1,0:T(8,128)S(1)}, f32[128,256]{1,0:T(8,128)S(1)}, u32[]{:S(2)}, u32[]{:S(2)}) collective-permute-start(f32[128,256]{1,0:T(8,128)S(1)} %get-tuple-element.70.refs_3_), channel_id=1, source_target_pairs={{1,2},{2,1},{3,4},{4,3},{5,6},{6,5},{7,0},{0,7},{9,10},{10,9},{11,... | collective-permute-start | bytes 393224 | tf_op jit(solution)/shard_map/ppermute | solution.py:153
  (34 other events, 30.0 us)
